TPU v7x, 32 devices: a whole 2x2x4 slice. The times are simulated.
32 devices in a mesh: groups: 2 (over y), seq: 4 (over z), mp: 2 (over x), sub: 2 (over core).
Axes of the slice: x: 2, y: 2, z: 4, core: 2. Of those that a mesh axis runs over, the one named last changes fastest.
Arguments:
- seq_in: bfloat16 [4096, 1536], P(('groups', 'seq'), ('mp', 'sub')), parts along dimension 0, may hold values from -48 to 48
- conv_gain: float32 [3, 1536], replicated, may hold values from 0.1 to 1.9
- conv_weight: bfloat16 [3, 3, 1536, 1536], P(None, None, None, ('mp', 'sub')), may hold values from -0.09375 to 0.09375
- w_q: bfloat16 [1536, 1024], P(None, 'mp'), may hold values from -0.102062073 to 0.102062073
- w_k: bfloat16 [1536, 1024], P(None, 'mp'), may hold values from -0.102062073 to 0.102062073
- w_v: bfloat16 [1536, 1024], P(None, 'mp'), may hold values from -0.15625 to 0.15625
- w_o: bfloat16 [1024, 1536], P('mp'), may hold values from -0.1875 to 0.1875
Outputs:
- seq_out: bfloat16 [4096, 1536], P(('groups', 'seq', 'sub'), 'mp'), parts along dimension 0
There are 2 independent parts, one for each index of `groups`. A program takes and returns all parts, laid end to end along the dimension named above; an argument that names none is the same for every part. Nothing has to cross between parts.
All inputs are finite; a program needn't handle non-finite values.
Results may differ from a plain program's by a relative error of at most 0.015.
Values may be sent and summed in bfloat16 or wider, within the bound.
No kernel may reach another device: no remote copies, remote signals or barrier semaphores. Data moves between devices by JAX's collectives and lax.ppermute only.
A program may use at most 128 MiB of HBM per device.

v0:
```python
import math
import jax
import jax.numpy as jnp
from jax import lax
from jax.sharding import PartitionSpec as P

HEAD = 128
LAYERS = 3
BINS_DEV = 512


def passed_along(x, axis, by):
    devices = lax.axis_size(axis)
    pairs = [(i, i + by) for i in range(devices) if 0 <= i + by < devices]
    return lax.ppermute(x, axis, pairs)


def tower_section(stream_shard, gain_row, weight_taps, dilation):
    rows_here = stream_shard.shape[0]
    gathered = lax.all_gather(stream_shard, ("mp", "sub"), axis=1, tiled=True)
    widened = gathered.astype(jnp.float32)
    normed = (
        widened * lax.rsqrt(jnp.mean(widened * widened, axis=1, keepdims=True) + 1e-06) * gain_row
    )
    hidden = jax.nn.gelu(normed).astype(jnp.bfloat16)
    tap_terms = jnp.einsum("rc,jco->jro", hidden, weight_taps, preferred_element_type=jnp.float32)
    span_rows = min(dilation, rows_here)
    hop_count = max(dilation // rows_here, 1)
    lower_part = passed_along(
        tap_terms[0, rows_here - span_rows :].astype(jnp.bfloat16), "seq", hop_count
    ).astype(jnp.float32)
    upper_part = passed_along(
        tap_terms[2, :span_rows].astype(jnp.bfloat16), "seq", -hop_count
    ).astype(jnp.float32)
    before = jnp.concatenate([lower_part, tap_terms[0, : rows_here - span_rows]], axis=0)
    after = jnp.concatenate([tap_terms[2, span_rows:], upper_part], axis=0)
    return (stream_shard.astype(jnp.float32) + before + tap_terms[1] + after).astype(jnp.bfloat16)


def per_device(seq_in, conv_gain, conv_weight, w_q, w_k, w_v, w_o):
    rows_here = seq_in.shape[0]
    dilations = (BINS_DEV // 4, BINS_DEV, 2 * BINS_DEV)
    stream = seq_in
    for section_index in range(LAYERS):
        stream = tower_section(
            stream, conv_gain[section_index], conv_weight[section_index], dilations[section_index]
        )
    query_rows = rows_here // lax.axis_size("sub")
    mp_width = w_o.shape[1] // lax.axis_size("mp")
    widest = lax.all_gather(stream, ("mp", "sub"), axis=1, tiled=True)
    query_inputs = lax.dynamic_slice_in_dim(
        widest, lax.axis_index("sub") * query_rows, query_rows, 0
    )
    residual_part = lax.dynamic_slice_in_dim(
        query_inputs, lax.axis_index("mp") * mp_width, mp_width, 1
    )
    heads_here = w_q.shape[1] // HEAD
    queries = (
        jnp.dot(query_inputs, w_q, preferred_element_type=jnp.float32)
        .astype(jnp.bfloat16)
        .reshape(query_rows, heads_here, HEAD)
    )
    keys = (
        jnp.dot(query_inputs, w_k, preferred_element_type=jnp.float32)
        .astype(jnp.bfloat16)
        .reshape(query_rows, heads_here, HEAD)
    )
    values = (
        jnp.dot(query_inputs, w_v, preferred_element_type=jnp.float32)
        .astype(jnp.bfloat16)
        .reshape(query_rows, heads_here, HEAD)
    )
    score_scale = 1.0 / math.sqrt(HEAD)
    running_top = jnp.full((heads_here, query_rows), -1e30, jnp.float32)
    running_numer = jnp.zeros((query_rows, heads_here, HEAD), jnp.float32)
    key_rows = lax.all_gather(keys, ("seq", "sub"), axis=0, tiled=True)
    value_rows = lax.all_gather(values, ("seq", "sub"), axis=0, tiled=True)
    scores = (
        jnp.einsum("qhe,khe->hqk", queries, key_rows, preferred_element_type=jnp.float32)
        * score_scale
    )
    new_top = jnp.maximum(running_top, jnp.max(scores, axis=-1))
    expw = jnp.exp(scores - new_top[:, :, None])
    factor = jnp.exp(running_top - new_top)
    new_denom = jnp.sum(expw, axis=-1)
    contrib = jnp.einsum(
        "hqk,khe->qhe", expw.astype(jnp.bfloat16), value_rows, preferred_element_type=jnp.float32
    )
    new_numer = running_numer * factor.T[:, :, None] + contrib
    attended = (
        (new_numer / new_denom.T[:, :, None])
        .astype(jnp.bfloat16)
        .reshape(query_rows, heads_here * HEAD)
    )
    column_weight = lax.all_to_all(w_o, "mp", split_axis=1, concat_axis=0, tiled=True)
    every_head = lax.all_gather(attended, "mp", axis=1, tiled=True)
    shares = jnp.dot(every_head, column_weight, preferred_element_type=jnp.float32)
    return (residual_part.astype(jnp.float32) + shares).astype(jnp.bfloat16)


def solution(mesh):
    placed = (
        P(("groups", "seq"), ("mp", "sub")),
        P(),
        P(None, None, None, ("mp", "sub")),
        P(None, "mp"),
        P(None, "mp"),
        P(None, "mp"),
        P("mp", None),
    )
    return jax.shard_map(
        per_device,
        mesh=mesh,
        in_specs=placed,
        out_specs=P(("groups", "seq", "sub"), "mp"),
        check_vma=False,
    )
```

profile of v0, /device:TPU:8, one launch (start us, length us, event | category | flops | bytes accessed | tf_op | source)
XLA Modules:
  0.0 252.6 jit_solution(15815357984765979070)
XLA Ops:
  8.2 21.5 %all-gather.7.cloned.1.call-done = bf16[512,1536]{1,0:T(8,128)(2,1)} async-done(((bf16[512,384]{1,0:T(8,128)(2,1)}), bf16[512,1536]{1,0:T(8,128)(2,1)}) %all-gather.7.cloned.1.call-update) | async-done | bytes 1572880 | tf_op jit(solution)/shard_map/all_gather | solution.py:20
  29.8 1.8 fusion.15
  31.6 5.6 %fusion.124 = (bf16[3,512,384]{2,1,0:T(8,128)(2,1)S(1)}, f32[3,512,384]{2,1,0:T(8,128)S(1)}) fusion(bf16[3,3,1536,384]{3,2,1,0:T(8,128)(2,1)} %param.9, bf16[512,1536]{1,0:T(8,128)(2,1)} %all-gather.7.cloned.1.call-done, f32[1536]{0:T(1024)S(1)} %get-tuple-element.6, f32[512]{0:T(512)S(1)} %add_rsqrt_fusion.2), kind=kOutput, calls=%fused_computation.142 | convolution fusion | flops 1821966336 | bytes 8658944 | tf_op jit(solution)/shard_map/rc,jco->jro/dot_general | solution.py:26
  37.2 3.5 %collective-permute-start = (bf16[128,384]{1,0:T(8,128)(2,1)S(1)}, bf16[128,384]{1,0:T(8,128)(2,1)S(1)}, u32[]{:S(2)}, u32[]{:S(2)}) collective-permute-start(bf16[128,384]{1,0:T(8,128)(2,1)S(1)} %get-tuple-element.15), channel_id=1, source_target_pairs={{0,4},{4,8},{8,12},{1,5},{5,9},{9,13},{2,6},{6,10},{10,14},{3,7},{... | collective-permute-start | bytes 294920 | tf_op jit(solution)/shard_map/ppermute | solution.py:15
  40.7 2.5 collective-permute-start.1
  44.2 3.1 %collective-permute-done.1 = bf16[128,384]{1,0:T(8,128)(2,1)S(1)} collective-permute-done((bf16[128,384]{1,0:T(8,128)(2,1)S(1)}, bf16[128,384]{1,0:T(8,128)(2,1)S(1)}, u32[]{:S(2)}, u32[]{:S(2)}) %collective-permute-start.1) | collective-permute-done | bytes 98336 | tf_op jit(solution)/shard_map/ppermute | solution.py:15
  48.3 18.8 %all-gather.9.cloned.1.call-done = bf16[512,1536]{1,0:T(8,128)(2,1)} async-done(((bf16[512,384]{1,0:T(8,128)(2,1)}), bf16[512,1536]{1,0:T(8,128)(2,1)}) %all-gather.9.cloned.1.call-update) | async-done | bytes 1572880 | tf_op jit(solution)/shard_map/all_gather | solution.py:20
  67.1 1.8 fusion.24
  68.9 5.6 %fusion.125 = (bf16[3,512,384]{2,1,0:T(8,128)(2,1)S(1)}, f32[3,512,384]{2,1,0:T(8,128)S(1)}) fusion(bf16[3,3,1536,384]{3,2,1,0:T(8,128)(2,1)} %param.9, bf16[512,1536]{1,0:T(8,128)(2,1)} %all-gather.9.cloned.1.call-done, f32[1536]{0:T(1024)S(1)} %get-tuple-element.7, f32[512]{0:T(512)S(1)} %add_rsqrt_fusion.1), kind=kOutput, calls=%fused_computation.143 | convolution fusion | flops 1821966336 | bytes 8658944 | tf_op jit(solution)/shard_map/rc,jco->jro/dot_general | solution.py:26
  74.7 3.4 %collective-permute-start.2 = (bf16[512,384]{1,0:T(8,128)(2,1)S(1)}, bf16[512,384]{1,0:T(8,128)(2,1)S(1)}, u32[]{:S(2)}, u32[]{:S(2)}) collective-permute-start(bf16[512,384]{1,0:T(8,128)(2,1)S(1)} %get-tuple-element.12), channel_id=1, source_target_pairs={{0,4},{4,8},{8,12},{1,5},{5,9},{9,13},{2,6},{6,10},{10,14},{3,7},{... | collective-permute-start | bytes 1179656 | tf_op jit(solution)/shard_map/ppermute | solution.py:15
  78.1 2.5 collective-permute-start.3
  80.6 7.3 %collective-permute-done.2 = bf16[512,384]{1,0:T(8,128)(2,1)S(1)} collective-permute-done((bf16[512,384]{1,0:T(8,128)(2,1)S(1)}, bf16[512,384]{1,0:T(8,128)(2,1)S(1)}, u32[]{:S(2)}, u32[]{:S(2)}) %collective-permute-start.2) | collective-permute-done | bytes 393248 | tf_op jit(solution)/shard_map/ppermute | solution.py:15
  87.8 3.1 %collective-permute-done.3 = bf16[512,384]{1,0:T(8,128)(2,1)S(1)} collective-permute-done((bf16[512,384]{1,0:T(8,128)(2,1)S(1)}, bf16[512,384]{1,0:T(8,128)(2,1)S(1)}, u32[]{:S(2)}, u32[]{:S(2)}) %collective-permute-start.3) | collective-permute-done | bytes 393248 | tf_op jit(solution)/shard_map/ppermute | solution.py:15
  92.0 18.8 %all-gather.11.cloned.1.call-done = bf16[512,1536]{1,0:T(8,128)(2,1)} async-done(((bf16[512,384]{1,0:T(8,128)(2,1)}), bf16[512,1536]{1,0:T(8,128)(2,1)}) %all-gather.11.cloned.1.call-update) | async-done | bytes 1572880 | tf_op jit(solution)/shard_map/all_gather | solution.py:20
  110.8 1.8 fusion.33
  112.6 5.6 %fusion.126 = (bf16[3,512,384]{2,1,0:T(8,128)(2,1)S(1)}, f32[3,512,384]{2,1,0:T(8,128)S(1)}) fusion(bf16[3,3,1536,384]{3,2,1,0:T(8,128)(2,1)} %param.9, bf16[512,1536]{1,0:T(8,128)(2,1)} %all-gather.11.cloned.1.call-done, f32[1536]{0:T(1024)S(1)} %get-tuple-element.5, f32[512]{0:T(512)S(1)} %add_rsqrt_fusion), kind=kOutput, calls=%fused_computation.144 | convolution fusion | flops 1821966336 | bytes 8658944 | tf_op jit(solution)/shard_map/rc,jco->jro/dot_general | solution.py:26
  118.4 4.3 %collective-permute-start.4 = (bf16[512,384]{1,0:T(8,128)(2,1)S(1)}, bf16[512,384]{1,0:T(8,128)(2,1)S(1)}, u32[]{:S(2)}, u32[]{:S(2)}) collective-permute-start(bf16[512,384]{1,0:T(8,128)(2,1)S(1)} %get-tuple-element.10), channel_id=1, source_target_pairs={{0,8},{4,12},{1,9},{5,13},{2,10},{6,14},{3,11},{7,15},{16,24},{20,... | collective-permute-start | bytes 1179656 | tf_op jit(solution)/shard_map/ppermute | solution.py:15
  124.0 15.8 %collective-permute-done.4 = bf16[512,384]{1,0:T(8,128)(2,1)S(1)} collective-permute-done((bf16[512,384]{1,0:T(8,128)(2,1)S(1)}, bf16[512,384]{1,0:T(8,128)(2,1)S(1)}, u32[]{:S(2)}, u32[]{:S(2)}) %collective-permute-start.4) | collective-permute-done | bytes 393248 | tf_op jit(solution)/shard_map/ppermute | solution.py:15
  140.9 22.0 %all-gather.13.cloned.1.call-done = bf16[512,1536]{1,0:T(8,128)(2,1)} async-done(((bf16[512,384]{1,0:T(8,128)(2,1)}), bf16[512,1536]{1,0:T(8,128)(2,1)}) %all-gather.13.cloned.1.call-update) | async-done | bytes 1572880 | tf_op jit(solution)/shard_map/all_gather | solution.py:50
  162.9 1.7 fusion.86
  165.6 2.2 convolution_convert_fusion
  170.3 3.7 %all-to-all-start = ((bf16[512,2,768]{0,2,1:T(8,128)(2,1)}), bf16[512,2,768]{0,2,1:T(8,128)(2,1)S(1)}, u32[]{:S(2)}, u32[]{:S(2)}) async-start(bf16[512,2,768]{0,2,1:T(8,128)(2,1)} %bitcast.118), calls=%async_computation | async-start | bytes 3145728 | tf_op jit(solution)/shard_map/all_to_all | solution.py:95
  174.0 19.9 %all-to-all-done = bf16[512,2,768]{0,2,1:T(8,128)(2,1)S(1)} async-done(((bf16[512,2,768]{0,2,1:T(8,128)(2,1)}), bf16[512,2,768]{0,2,1:T(8,128)(2,1)S(1)}, u32[]{:S(2)}, u32[]{:S(2)}) %all-to-all-start) | async-done | bytes 1572896 | tf_op jit(solution)/shard_map/all_to_all | solution.py:95
  193.9 1.6 copy.18
  195.5 2.2 fusion.85
  197.8 2.9 %multiply_reduce_fusion = (f32[4,256]{1,0:T(4,128)S(1)}, f32[4,256,2048]{2,1,0:T(8,128)S(1)}) fusion(bf16[2048,4,128]{2,0,1:T(8,128)(2,1)} %all-gather.15.cloned.1.call-done, bf16[32,4,8,128]{3,2,1,0:T(8,128)(2,1)S(1)} %fusion.85), kind=kOutput, calls=%fused_computation.1 | convolution fusion | flops 541064192 | bytes 10752000 | tf_op jit(solution)/shard_map/qhe,khe->hqk/dot_general | solution.py:79
  200.7 3.2 %copy-done.1 = f32[4,256,2048]{2,1,0:T(8,128)} copy-done((f32[4,256,2048]{2,1,0:T(8,128)}, f32[4,256,2048]{2,1,0:T(8,128)S(1)}, u32[]{:S(2)}) %copy-start.1) | copy-done | bytes 8388632
  204.0 1.6 fusion
  205.6 22.7 %all-gather.17.cloned.1.call-done = bf16[2048,4,128]{0,2,1:T(8,128)(2,1)} async-done(((bf16[256,4,128]{0,2,1:T(8,128)(2,1)}), bf16[2048,4,128]{0,2,1:T(8,128)(2,1)}) %all-gather.17.cloned.1.call-update) | async-done | bytes 2097168 | tf_op jit(solution)/shard_map/all_gather | solution.py:77
  228.3 5.9 %fusion.90 = bf16[256,4,128]{0,2,1:T(8,128)(2,1)S(1)} fusion(bf16[2048,4,128]{0,2,1:T(8,128)(2,1)} %all-gather.17.cloned.1.call-done, f32[4,256,2048]{2,1,0:T(8,128)} %copy-done.1, f32[4,256]{1,0:T(4,128)S(1)} %get-tuple-element.17, f32[256,4]{0,1:T(4,128)S(1)} %bitcast.123, f32[256,4]{0,1:T(4,128)S(1)} %get-tuple-element.16), kind=kOutput, calls=%fused_computation.89 | convolution fusion | flops 543555584 | bytes 10760192 | tf_op jit(solution)/shard_map/hqk,khe->qhe/dot_general | solution.py:86
  234.2 9.1 %all_gather.27 = bf16[256,1024]{0,1:T(8,128)(2,1)S(1)} all-gather(bf16[256,512]{0,1:T(8,128)(2,1)S(1)} %bitcast.122), channel_id=1, replica_groups=mesh['groups'=2,'seq'=4,'mp'=2,'sub'=2] {'mp'}, dimensions={1}, use_global_device_ids=true | all-gather | bytes 786432 | tf_op jit(solution)/shard_map/all_gather | solution.py:96
  243.4 2.4 fusion.78
  (46 shorter events, 10.7 us)
Async XLA Ops:
  6.5 156.4 %copy-start = (bf16[1536,512]{1,0:T(8,128)(2,1)S(1)}, bf16[1536,512]{1,0:T(8,128)(2,1)}, u32[]{:S(2)}) copy-start(bf16[1536,512]{1,0:T(8,128)(2,1)} %param.11) | copy-start | bytes 4718596
  6.5 23.2 %all-gather.7.cloned.1.call-start = ((), (), s32[]{:S(2)}) async-start(), calls=%async_computation.1 | async-start | bytes 1966080 | tf_op jit(solution)/shard_map/all_gather | solution.py:20
  7.3 59.9 %all-gather.9.cloned.1.call-start = ((), (), s32[]{:S(2)}) async-start(), calls=%async_computation.2 | async-start | bytes 1966080 | tf_op jit(solution)/shard_map/all_gather | solution.py:20
  37.1 10.1 %copy-start.6 = (bf16[512,384]{1,0:T(8,128)(2,1)S(1)}, bf16[512,384]{1,0:T(8,128)(2,1)}, u32[]{:S(2)}) copy-start(bf16[512,384]{1,0:T(8,128)(2,1)} %param.7) | copy-start | bytes 1179652
  37.2 7.0 %collective-permute-start = (bf16[128,384]{1,0:T(8,128)(2,1)S(1)}, bf16[128,384]{1,0:T(8,128)(2,1)S(1)}, u32[]{:S(2)}, u32[]{:S(2)}) collective-permute-start(bf16[128,384]{1,0:T(8,128)(2,1)S(1)} %get-tuple-element.15), channel_id=1, source_target_pairs={{0,4},{4,8},{8,12},{1,5},{5,9},{9,13},{2,6},{6,10},{10,14},{3,7},{... | collective-permute-start | bytes 294920 | tf_op jit(solution)/shard_map/ppermute | solution.py:15
  40.7 6.6 %collective-permute-start.1 = (bf16[128,384]{1,0:T(8,128)(2,1)S(1)}, bf16[128,384]{1,0:T(8,128)(2,1)S(1)}, u32[]{:S(2)}, u32[]{:S(2)}) collective-permute-start(bf16[128,384]{1,0:T(8,128)(2,1)S(1)} %get-tuple-element.14), channel_id=1, source_target_pairs={{4,0},{8,4},{12,8},{5,1},{9,5},{13,9},{6,2},{10,6},{14,10},{7,3},{... | collective-permute-start | bytes 294920 | tf_op jit(solution)/shard_map/ppermute | solution.py:15
  48.3 62.5 %all-gather.11.cloned.1.call-start = ((), (), s32[]{:S(2)}) async-start(), calls=%async_computation.3 | async-start | bytes 1966080 | tf_op jit(solution)/shard_map/all_gather | solution.py:20
  68.9 22.0 %copy-start.3 = (bf16[512,384]{1,0:T(8,128)(2,1)S(1)}, bf16[512,384]{1,0:T(8,128)(2,1)}, u32[]{:S(2)}) copy-start(bf16[512,384]{1,0:T(8,128)(2,1)} %fusion.101) | copy-start | bytes 1179652
  74.7 13.1 %collective-permute-start.2 = (bf16[512,384]{1,0:T(8,128)(2,1)S(1)}, bf16[512,384]{1,0:T(8,128)(2,1)S(1)}, u32[]{:S(2)}, u32[]{:S(2)}) collective-permute-start(bf16[512,384]{1,0:T(8,128)(2,1)S(1)} %get-tuple-element.12), channel_id=1, source_target_pairs={{0,4},{4,8},{8,12},{1,5},{5,9},{9,13},{2,6},{6,10},{10,14},{3,7},{... | collective-permute-start | bytes 1179656 | tf_op jit(solution)/shard_map/ppermute | solution.py:15
  78.1 12.9 %collective-permute-start.3 = (bf16[512,384]{1,0:T(8,128)(2,1)S(1)}, bf16[512,384]{1,0:T(8,128)(2,1)S(1)}, u32[]{:S(2)}, u32[]{:S(2)}) collective-permute-start(bf16[512,384]{1,0:T(8,128)(2,1)S(1)} %get-tuple-element.13), channel_id=1, source_target_pairs={{4,0},{8,4},{12,8},{5,1},{9,5},{13,9},{6,2},{10,6},{14,10},{7,3},{... | collective-permute-start | bytes 1179656 | tf_op jit(solution)/shard_map/ppermute | solution.py:15
  91.9 71.0 %all-gather.13.cloned.1.call-start = ((), (), s32[]{:S(2)}) async-start(), calls=%async_computation.4 | async-start | bytes 1966080 | tf_op jit(solution)/shard_map/all_gather | solution.py:50
  112.6 27.2 %copy-start.4 = (bf16[512,384]{1,0:T(8,128)(2,1)S(1)}, bf16[512,384]{1,0:T(8,128)(2,1)}, u32[]{:S(2)}) copy-start(bf16[512,384]{1,0:T(8,128)(2,1)} %fusion.98) | copy-start | bytes 1179652
  118.4 21.5 %collective-permute-start.4 = (bf16[512,384]{1,0:T(8,128)(2,1)S(1)}, bf16[512,384]{1,0:T(8,128)(2,1)S(1)}, u32[]{:S(2)}, u32[]{:S(2)}) collective-permute-start(bf16[512,384]{1,0:T(8,128)(2,1)S(1)} %get-tuple-element.10), channel_id=1, source_target_pairs={{0,8},{4,12},{1,9},{5,13},{2,10},{6,14},{3,11},{7,15},{16,24},{20,... | collective-permute-start | bytes 1179656 | tf_op jit(solution)/shard_map/ppermute | solution.py:15
  122.7 17.1 %collective-permute-start.5 = (bf16[512,384]{1,0:T(8,128)(2,1)S(1)}, bf16[512,384]{1,0:T(8,128)(2,1)S(1)}, u32[]{:S(2)}, u32[]{:S(2)}) collective-permute-start(bf16[512,384]{1,0:T(8,128)(2,1)S(1)} %get-tuple-element.11), channel_id=1, source_target_pairs={{8,0},{12,4},{9,1},{13,5},{10,2},{14,6},{11,3},{15,7},{24,16},{28,... | collective-permute-start | bytes 1179656 | tf_op jit(solution)/shard_map/ppermute | solution.py:15
  140.8 57.0 %all-gather.15.cloned.1.call-start = ((), (), s32[]{:S(2)}) async-start(), calls=%async_computation.5 | async-start | bytes 2359296 | tf_op jit(solution)/shard_map/all_gather | solution.py:76
  140.9 27.8 %copy-start.5 = (bf16[512,1536]{1,0:T(8,128)(2,1)S(1)}, bf16[512,1536]{1,0:T(8,128)(2,1)}, u32[]{:S(2)}) copy-start(bf16[512,1536]{1,0:T(8,128)(2,1)} %param.13) | copy-start | bytes 4718596
  165.4 62.9 %all-gather.17.cloned.1.call-start = ((), (), s32[]{:S(2)}) async-start(), calls=%async_computation.6 | async-start | bytes 2359296 | tf_op jit(solution)/shard_map/all_gather | solution.py:77
  170.3 23.6 %all-to-all-start = ((bf16[512,2,768]{0,2,1:T(8,128)(2,1)}), bf16[512,2,768]{0,2,1:T(8,128)(2,1)S(1)}, u32[]{:S(2)}, u32[]{:S(2)}) async-start(bf16[512,2,768]{0,2,1:T(8,128)(2,1)} %bitcast.118), calls=%async_computation | async-start | bytes 3145728 | tf_op jit(solution)/shard_map/all_to_all | solution.py:95
  200.7 3.2 %copy-start.1 = (f32[4,256,2048]{2,1,0:T(8,128)}, f32[4,256,2048]{2,1,0:T(8,128)S(1)}, u32[]{:S(2)}) copy-start(f32[4,256,2048]{2,1,0:T(8,128)S(1)} %get-tuple-element.25) | copy-start | bytes 25165828
  228.3 15.1 %copy-start.2 = (bf16[2,512,768]{2,1,0:T(8,128)(2,1)S(1)}, bf16[2,512,768]{2,1,0:T(8,128)(2,1)}, u32[]{:S(2)}) copy-start(bf16[2,512,768]{2,1,0:T(8,128)(2,1)} %copy.18) | copy-start | bytes 4718596
Sparse Core Ops, SparseCore 0:
  8.9 20.7 all-gather.6
  48.4 18.7 all-gather.8
  92.1 18.7 all-gather.10
  140.9 21.9 all-gather.12
  165.5 29.0 all-gather.14
  196.1 32.1 all-gather.16
where the time goes:
time: 253 us
  waiting for transfers between devices  155 us (61%)
  matrix products  34.3 us (14%)
  starting transfers between devices  21.6 us (9%)
  between operations  13.7 us (5%)
  other arithmetic  9.91 us (4%)
  local copies, waits for them, and re-layouts  9.22 us (4%)
  blocking collectives  9.14 us (4%)
    all_gather x3, waiting for transfers between devices, tower_section(): gathered = lax.all_gather(stream_shard, ('mp', 'sub'), axis=1, tiled=True)  59.2 us
    ppermute x6, waiting for transfers between devices, passed_along(): return lax.ppermute(x, axis, pairs)  30.2 us
    all_gather x1, waiting for transfers between devices, per_device(): value_rows = lax.all_gather(values, ('seq', 'sub'), axis=0, tiled=True)  22.7 us
    all_gather x1, waiting for transfers between devices, per_device(): widest = lax.all_gather(stream, ('mp', 'sub'), axis=1, tiled=True)  22 us
    all_to_all x1, waiting for transfers between devices, per_device(): lax.all_to_all(w_o, 'mp', split_axis=1, concat_axis=0, tiled=True)  19.9 us
    ppermute x6, starting transfers between devices, passed_along(): return lax.ppermute(x, axis, pairs)  17.5 us
    dot_general x3, matrix products, tower_section(): jnp.einsum('rc,jco->jro', hidden, weight_taps, preferred_element_type=jnp...  16.9 us
    all_gather x1, blocking collectives, per_device(): every_head = lax.all_gather(attended, 'mp', axis=1, tiled=True)  9.14 us
  transfers between devices with their start and end apart: 13, of which 11 were waited for; matrix products, arithmetic and copies ran while one was open for 6% of the time, Pallas kernels for 0%

commit v1 on v0

--- a/solution.py
+++ b/solution.py
@@ -73,8 +73,13 @@
     score_scale = 1.0 / math.sqrt(HEAD)
     running_top = jnp.full((heads_here, query_rows), -1e30, jnp.float32)
     running_numer = jnp.zeros((query_rows, heads_here, HEAD), jnp.float32)
-    key_rows = lax.all_gather(keys, ("seq", "sub"), axis=0, tiled=True)
-    value_rows = lax.all_gather(values, ("seq", "sub"), axis=0, tiled=True)
+    key_rows, value_rows = jnp.split(
+        lax.all_gather(
+            jnp.concatenate([keys, values], axis=1), axis_name=("seq", "sub"), axis=0, tiled=True
+        ),
+        [keys.shape[1]],
+        axis=1,
+    )
     scores = (
         jnp.einsum("qhe,khe->hqk", queries, key_rows, preferred_element_type=jnp.float32)
         * score_scale

time: 253 us -> 243 us (0.960); the launches traced: 253 us -> 239 us
  waiting for transfers between devices: 155 us -> 149 us
  local copies, waits for them, and re-layouts: 9.22 us -> 4.99 us
  matrix products: 34.3 us -> 30.4 us
    all_gather x2 -> x1, waiting for transfers between devices: 22.7 us -> 16.8 us  [per_device(): lax.all_gather(jnp.concatenate([keys, values], axis=1), axis_name=('seq',...]
    dot_general x1, matrix products: 5.95 us -> 1.99 us  [per_device(): jnp.einsum('hqk,khe->qhe', expw.astype(jnp.bfloat16), value_rows, preferr...]
    unnamed x15, local copies, waits for them, and re-layouts: 4.83 us -> 2.16 us
  transfers between devices with their start and end apart: 13 -> 12, of which waited for: 11 -> 11; matrix products, arithmetic and copies ran while one was open for 6% -> 3% of each run, Pallas kernels for 0% -> 0%
where the time goes in v1:
time: 243 us; the launch traced here: 239 us
  waiting for transfers between devices  149 us (61%)
  matrix products  30.4 us (13%)
  starting transfers between devices  21.5 us (9%)
  between operations  13.4 us (6%)
  other arithmetic  10.8 us (4%)
  blocking collectives  9.13 us (4%)
  local copies, waits for them, and re-layouts  4.99 us (2%)
    all_gather x3, waiting for transfers between devices, tower_section(): gathered = lax.all_gather(stream_shard, ('mp', 'sub'), axis=1, tiled=True)  59.2 us
    ppermute x6, waiting for transfers between devices, passed_along(): return lax.ppermute(x, axis, pairs)  30.2 us
    all_gather x1, waiting for transfers between devices, per_device(): widest = lax.all_gather(stream, ('mp', 'sub'), axis=1, tiled=True)  21.8 us
    all_to_all x1, waiting for transfers between devices, per_device(): lax.all_to_all(w_o, 'mp', split_axis=1, concat_axis=0, tiled=True)  19.9 us
    ppermute x6, starting transfers between devices, passed_along(): return lax.ppermute(x, axis, pairs)  17.5 us
    dot_general x3, matrix products, tower_section(): jnp.einsum('rc,jco->jro', hidden, weight_taps, preferred_element_type=jnp...  16.9 us
    all_gather x1, waiting for transfers between devices, per_device(): lax.all_gather(jnp.concatenate([keys, values], axis=1), axis_name=('seq',...  16.8 us
    all_gather x1, blocking collectives, per_device(): every_head = lax.all_gather(attended, 'mp', axis=1, tiled=True)  9.13 us
  transfers between devices with their start and end apart: 12, of which 11 were waited for; matrix products, arithmetic and copies ran while one was open for 3% of the time, Pallas kernels for 0%

profile of v1, /device:TPU:8, one launch (start us, length us, event | category | flops | bytes accessed | tf_op | source)
XLA Modules:
  0.0 238.9 jit_solution(10739785744846522790)
XLA Ops:
  8.2 21.5 %all-gather.6.cloned.1.call-done = bf16[512,1536]{1,0:T(8,128)(2,1)} async-done(((bf16[512,384]{1,0:T(8,128)(2,1)}), bf16[512,1536]{1,0:T(8,128)(2,1)}) %all-gather.6.cloned.1.call-update) | async-done | bytes 1572880 | tf_op jit(solution)/shard_map/all_gather | solution.py:20
  29.8 1.8 fusion.15
  31.6 5.6 %fusion.126 = (bf16[3,512,384]{2,1,0:T(8,128)(2,1)S(1)}, f32[3,512,384]{2,1,0:T(8,128)S(1)}) fusion(bf16[3,3,1536,384]{3,2,1,0:T(8,128)(2,1)} %param.9, bf16[512,1536]{1,0:T(8,128)(2,1)} %all-gather.6.cloned.1.call-done, f32[1536]{0:T(1024)S(1)} %get-tuple-element.6, f32[512]{0:T(512)S(1)} %add_rsqrt_fusion.2), kind=kOutput, calls=%fused_computation.146 | convolution fusion | flops 1821966336 | bytes 8658944 | tf_op jit(solution)/shard_map/rc,jco->jro/dot_general | solution.py:26
  37.2 3.5 %collective-permute-start = (bf16[128,384]{1,0:T(8,128)(2,1)S(1)}, bf16[128,384]{1,0:T(8,128)(2,1)S(1)}, u32[]{:S(2)}, u32[]{:S(2)}) collective-permute-start(bf16[128,384]{1,0:T(8,128)(2,1)S(1)} %get-tuple-element.15), channel_id=1, source_target_pairs={{0,4},{4,8},{8,12},{1,5},{5,9},{9,13},{2,6},{6,10},{10,14},{3,7},{... | collective-permute-start | bytes 294920 | tf_op jit(solution)/shard_map/ppermute | solution.py:15
  40.7 2.5 %collective-permute-start.1 = (bf16[128,384]{1,0:T(8,128)(2,1)S(1)}, bf16[128,384]{1,0:T(8,128)(2,1)S(1)}, u32[]{:S(2)}, u32[]{:S(2)}) collective-permute-start(bf16[128,384]{1,0:T(8,128)(2,1)S(1)} %get-tuple-element.14), channel_id=1, source_target_pairs={{4,0},{8,4},{12,8},{5,1},{9,5},{13,9},{6,2},{10,6},{14,10},{7,3},{... | collective-permute-start | bytes 294920 | tf_op jit(solution)/shard_map/ppermute | solution.py:15
  44.2 3.1 %collective-permute-done.1 = bf16[128,384]{1,0:T(8,128)(2,1)S(1)} collective-permute-done((bf16[128,384]{1,0:T(8,128)(2,1)S(1)}, bf16[128,384]{1,0:T(8,128)(2,1)S(1)}, u32[]{:S(2)}, u32[]{:S(2)}) %collective-permute-start.1) | collective-permute-done | bytes 98336 | tf_op jit(solution)/shard_map/ppermute | solution.py:15
  48.3 18.8 %all-gather.8.cloned.1.call-done = bf16[512,1536]{1,0:T(8,128)(2,1)} async-done(((bf16[512,384]{1,0:T(8,128)(2,1)}), bf16[512,1536]{1,0:T(8,128)(2,1)}) %all-gather.8.cloned.1.call-update) | async-done | bytes 1572880 | tf_op jit(solution)/shard_map/all_gather | solution.py:20
  67.1 1.8 fusion.24
  68.9 5.6 %fusion.127 = (bf16[3,512,384]{2,1,0:T(8,128)(2,1)S(1)}, f32[3,512,384]{2,1,0:T(8,128)S(1)}) fusion(bf16[3,3,1536,384]{3,2,1,0:T(8,128)(2,1)} %param.9, bf16[512,1536]{1,0:T(8,128)(2,1)} %all-gather.8.cloned.1.call-done, f32[1536]{0:T(1024)S(1)} %get-tuple-element.7, f32[512]{0:T(512)S(1)} %add_rsqrt_fusion.1), kind=kOutput, calls=%fused_computation.147 | convolution fusion | flops 1821966336 | bytes 8658944 | tf_op jit(solution)/shard_map/rc,jco->jro/dot_general | solution.py:26
  74.7 3.4 %collective-permute-start.2 = (bf16[512,384]{1,0:T(8,128)(2,1)S(1)}, bf16[512,384]{1,0:T(8,128)(2,1)S(1)}, u32[]{:S(2)}, u32[]{:S(2)}) collective-permute-start(bf16[512,384]{1,0:T(8,128)(2,1)S(1)} %get-tuple-element.12), channel_id=1, source_target_pairs={{0,4},{4,8},{8,12},{1,5},{5,9},{9,13},{2,6},{6,10},{10,14},{3,7},{... | collective-permute-start | bytes 1179656 | tf_op jit(solution)/shard_map/ppermute | solution.py:15
  78.1 2.5 %collective-permute-start.3 = (bf16[512,384]{1,0:T(8,128)(2,1)S(1)}, bf16[512,384]{1,0:T(8,128)(2,1)S(1)}, u32[]{:S(2)}, u32[]{:S(2)}) collective-permute-start(bf16[512,384]{1,0:T(8,128)(2,1)S(1)} %get-tuple-element.13), channel_id=1, source_target_pairs={{4,0},{8,4},{12,8},{5,1},{9,5},{13,9},{6,2},{10,6},{14,10},{7,3},{... | collective-permute-start | bytes 1179656 | tf_op jit(solution)/shard_map/ppermute | solution.py:15
  80.6 7.3 %collective-permute-done.2 = bf16[512,384]{1,0:T(8,128)(2,1)S(1)} collective-permute-done((bf16[512,384]{1,0:T(8,128)(2,1)S(1)}, bf16[512,384]{1,0:T(8,128)(2,1)S(1)}, u32[]{:S(2)}, u32[]{:S(2)}) %collective-permute-start.2) | collective-permute-done | bytes 393248 | tf_op jit(solution)/shard_map/ppermute | solution.py:15
  87.8 3.1 %collective-permute-done.3 = bf16[512,384]{1,0:T(8,128)(2,1)S(1)} collective-permute-done((bf16[512,384]{1,0:T(8,128)(2,1)S(1)}, bf16[512,384]{1,0:T(8,128)(2,1)S(1)}, u32[]{:S(2)}, u32[]{:S(2)}) %collective-permute-start.3) | collective-permute-done | bytes 393248 | tf_op jit(solution)/shard_map/ppermute | solution.py:15
  92.0 18.8 %all-gather.10.cloned.1.call-done = bf16[512,1536]{1,0:T(8,128)(2,1)} async-done(((bf16[512,384]{1,0:T(8,128)(2,1)}), bf16[512,1536]{1,0:T(8,128)(2,1)}) %all-gather.10.cloned.1.call-update) | async-done | bytes 1572880 | tf_op jit(solution)/shard_map/all_gather | solution.py:20
  110.8 1.8 fusion.33
  112.6 5.6 %fusion.128 = (bf16[3,512,384]{2,1,0:T(8,128)(2,1)S(1)}, f32[3,512,384]{2,1,0:T(8,128)S(1)}) fusion(bf16[3,3,1536,384]{3,2,1,0:T(8,128)(2,1)} %param.9, bf16[512,1536]{1,0:T(8,128)(2,1)} %all-gather.10.cloned.1.call-done, f32[1536]{0:T(1024)S(1)} %get-tuple-element.5, f32[512]{0:T(512)S(1)} %add_rsqrt_fusion), kind=kOutput, calls=%fused_computation.148 | convolution fusion | flops 1821966336 | bytes 8658944 | tf_op jit(solution)/shard_map/rc,jco->jro/dot_general | solution.py:26
  118.4 4.3 %collective-permute-start.4 = (bf16[512,384]{1,0:T(8,128)(2,1)S(1)}, bf16[512,384]{1,0:T(8,128)(2,1)S(1)}, u32[]{:S(2)}, u32[]{:S(2)}) collective-permute-start(bf16[512,384]{1,0:T(8,128)(2,1)S(1)} %get-tuple-element.10), channel_id=1, source_target_pairs={{0,8},{4,12},{1,9},{5,13},{2,10},{6,14},{3,11},{7,15},{16,24},{20,... | collective-permute-start | bytes 1179656 | tf_op jit(solution)/shard_map/ppermute | solution.py:15
  124.0 15.8 %collective-permute-done.4 = bf16[512,384]{1,0:T(8,128)(2,1)S(1)} collective-permute-done((bf16[512,384]{1,0:T(8,128)(2,1)S(1)}, bf16[512,384]{1,0:T(8,128)(2,1)S(1)}, u32[]{:S(2)}, u32[]{:S(2)}) %collective-permute-start.4) | collective-permute-done | bytes 393248 | tf_op jit(solution)/shard_map/ppermute | solution.py:15
  141.1 21.8 %all-gather.12.cloned.1.call-done = bf16[512,1536]{1,0:T(8,128)(2,1)} async-done(((bf16[512,384]{1,0:T(8,128)(2,1)}), bf16[512,1536]{1,0:T(8,128)(2,1)}) %all-gather.12.cloned.1.call-update) | async-done | bytes 1572880 | tf_op jit(solution)/shard_map/all_gather | solution.py:50
  162.9 1.7 fusion.94
  164.6 2.3 fusion.95
  167.9 1.6 copy.20
  169.5 3.7 %all-to-all-start = ((bf16[512,2,768]{0,2,1:T(8,128)(2,1)}), bf16[512,2,768]{0,2,1:T(8,128)(2,1)S(1)}, u32[]{:S(2)}, u32[]{:S(2)}) async-start(bf16[512,2,768]{0,2,1:T(8,128)(2,1)} %bitcast.119), calls=%async_computation | async-start | bytes 3145728 | tf_op jit(solution)/shard_map/all_to_all | solution.py:100
  173.2 19.9 %all-to-all-done = bf16[512,2,768]{0,2,1:T(8,128)(2,1)S(1)} async-done(((bf16[512,2,768]{0,2,1:T(8,128)(2,1)}), bf16[512,2,768]{0,2,1:T(8,128)(2,1)S(1)}, u32[]{:S(2)}, u32[]{:S(2)}) %all-to-all-start) | async-done | bytes 1572896 | tf_op jit(solution)/shard_map/all_to_all | solution.py:100
  193.1 1.6 copy.21
  194.7 2.2 fusion.93
  196.9 16.8 %all-gather.14.cloned.1.call-done = bf16[2048,8,128]{2,0,1:T(8,128)(2,1)} async-done(((bf16[256,8,128]{2,0,1:T(8,128)(2,1)}), bf16[2048,8,128]{2,0,1:T(8,128)(2,1)}) %all-gather.14.cloned.1.call-update) | async-done | bytes 4194320 | tf_op jit(solution)/shard_map/all_gather | solution.py:77
  213.7 2.9 %multiply_reduce_fusion = (f32[4,256]{1,0:T(4,128)S(1)}, f32[4,256,2048]{2,1,0:T(8,128)S(1)}) fusion(bf16[2048,8,128]{2,0,1:T(8,128)(2,1)} %all-gather.14.cloned.1.call-done, bf16[32,4,8,128]{3,2,1,0:T(8,128)(2,1)S(1)} %fusion.93), kind=kOutput, calls=%fused_computation.1 | convolution fusion | flops 541064192 | bytes 10752000 | tf_op jit(solution)/shard_map/qhe,khe->hqk/dot_general | solution.py:84
  216.6 1.6 fusion
  218.8 2.0 fusion.90
  220.8 9.1 %all_gather.23 = bf16[256,1024]{0,1:T(8,128)(2,1)S(1)} all-gather(bf16[256,512]{0,1:T(8,128)(2,1)S(1)} %bitcast.121), channel_id=1, replica_groups=mesh['groups'=2,'seq'=4,'mp'=2,'sub'=2] {'mp'}, dimensions={1}, use_global_device_ids=true | all-gather | bytes 786432 | tf_op jit(solution)/shard_map/all_gather | solution.py:101
  229.9 2.4 %fusion.80 = bf16[256,768]{1,0:T(8,128)(2,1)} fusion(bf16[256,1024]{0,1:T(8,128)(2,1)S(1)} %all_gather.23, bf16[1024,768]{1,0:T(8,128)(2,1)S(1)} %bitcast.120, bf16[512,1536]{1,0:T(8,128)(2,1)} %all-gather.12.cloned.1.call-done, s32[]{:T(128)S(6)} %select_n.11, s32[]{:T(128)S(6)} %select_n.13), kind=kOutput, calls=%fused_computation.82 | convolution fusion | flops 403243008 | bytes 2883592 | tf_op jit(solution)/shard_map/dot_general | solution.py:102
  (43 shorter events, 8.9 us)
Async XLA Ops:
  6.5 156.4 %copy-start = (bf16[1536,512]{1,0:T(8,128)(2,1)S(1)}, bf16[1536,512]{1,0:T(8,128)(2,1)}, u32[]{:S(2)}) copy-start(bf16[1536,512]{1,0:T(8,128)(2,1)} %param.11) | copy-start | bytes 4718596
  6.5 23.2 %all-gather.6.cloned.1.call-start = ((), (), s32[]{:S(2)}) async-start(), calls=%async_computation.1 | async-start | bytes 1966080 | tf_op jit(solution)/shard_map/all_gather | solution.py:20
  7.3 59.9 %all-gather.8.cloned.1.call-start = ((), (), s32[]{:S(2)}) async-start(), calls=%async_computation.2 | async-start | bytes 1966080 | tf_op jit(solution)/shard_map/all_gather | solution.py:20
  37.1 10.1 %copy-start.5 = (bf16[512,384]{1,0:T(8,128)(2,1)S(1)}, bf16[512,384]{1,0:T(8,128)(2,1)}, u32[]{:S(2)}) copy-start(bf16[512,384]{1,0:T(8,128)(2,1)} %param.7) | copy-start | bytes 1179652
  37.2 7.0 %collective-permute-start = (bf16[128,384]{1,0:T(8,128)(2,1)S(1)}, bf16[128,384]{1,0:T(8,128)(2,1)S(1)}, u32[]{:S(2)}, u32[]{:S(2)}) collective-permute-start(bf16[128,384]{1,0:T(8,128)(2,1)S(1)} %get-tuple-element.15), channel_id=1, source_target_pairs={{0,4},{4,8},{8,12},{1,5},{5,9},{9,13},{2,6},{6,10},{10,14},{3,7},{... | collective-permute-start | bytes 294920 | tf_op jit(solution)/shard_map/ppermute | solution.py:15
  40.7 6.6 %collective-permute-start.1 = (bf16[128,384]{1,0:T(8,128)(2,1)S(1)}, bf16[128,384]{1,0:T(8,128)(2,1)S(1)}, u32[]{:S(2)}, u32[]{:S(2)}) collective-permute-start(bf16[128,384]{1,0:T(8,128)(2,1)S(1)} %get-tuple-element.14), channel_id=1, source_target_pairs={{4,0},{8,4},{12,8},{5,1},{9,5},{13,9},{6,2},{10,6},{14,10},{7,3},{... | collective-permute-start | bytes 294920 | tf_op jit(solution)/shard_map/ppermute | solution.py:15
  48.3 62.5 %all-gather.10.cloned.1.call-start = ((), (), s32[]{:S(2)}) async-start(), calls=%async_computation.3 | async-start | bytes 1966080 | tf_op jit(solution)/shard_map/all_gather | solution.py:20
  68.9 22.0 %copy-start.2 = (bf16[512,384]{1,0:T(8,128)(2,1)S(1)}, bf16[512,384]{1,0:T(8,128)(2,1)}, u32[]{:S(2)}) copy-start(bf16[512,384]{1,0:T(8,128)(2,1)} %fusion.104) | copy-start | bytes 1179652
  74.7 13.1 %collective-permute-start.2 = (bf16[512,384]{1,0:T(8,128)(2,1)S(1)}, bf16[512,384]{1,0:T(8,128)(2,1)S(1)}, u32[]{:S(2)}, u32[]{:S(2)}) collective-permute-start(bf16[512,384]{1,0:T(8,128)(2,1)S(1)} %get-tuple-element.12), channel_id=1, source_target_pairs={{0,4},{4,8},{8,12},{1,5},{5,9},{9,13},{2,6},{6,10},{10,14},{3,7},{... | collective-permute-start | bytes 1179656 | tf_op jit(solution)/shard_map/ppermute | solution.py:15
  78.1 12.9 %collective-permute-start.3 = (bf16[512,384]{1,0:T(8,128)(2,1)S(1)}, bf16[512,384]{1,0:T(8,128)(2,1)S(1)}, u32[]{:S(2)}, u32[]{:S(2)}) collective-permute-start(bf16[512,384]{1,0:T(8,128)(2,1)S(1)} %get-tuple-element.13), channel_id=1, source_target_pairs={{4,0},{8,4},{12,8},{5,1},{9,5},{13,9},{6,2},{10,6},{14,10},{7,3},{... | collective-permute-start | bytes 1179656 | tf_op jit(solution)/shard_map/ppermute | solution.py:15
  91.9 71.0 %all-gather.12.cloned.1.call-start = ((), (), s32[]{:S(2)}) async-start(), calls=%async_computation.4 | async-start | bytes 1966080 | tf_op jit(solution)/shard_map/all_gather | solution.py:50
  112.6 27.2 %copy-start.3 = (bf16[512,384]{1,0:T(8,128)(2,1)S(1)}, bf16[512,384]{1,0:T(8,128)(2,1)}, u32[]{:S(2)}) copy-start(bf16[512,384]{1,0:T(8,128)(2,1)} %fusion.101) | copy-start | bytes 1179652
  118.4 21.5 %collective-permute-start.4 = (bf16[512,384]{1,0:T(8,128)(2,1)S(1)}, bf16[512,384]{1,0:T(8,128)(2,1)S(1)}, u32[]{:S(2)}, u32[]{:S(2)}) collective-permute-start(bf16[512,384]{1,0:T(8,128)(2,1)S(1)} %get-tuple-element.10), channel_id=1, source_target_pairs={{0,8},{4,12},{1,9},{5,13},{2,10},{6,14},{3,11},{7,15},{16,24},{20,... | collective-permute-start | bytes 1179656 | tf_op jit(solution)/shard_map/ppermute | solution.py:15
  122.7 17.1 %collective-permute-start.5 = (bf16[512,384]{1,0:T(8,128)(2,1)S(1)}, bf16[512,384]{1,0:T(8,128)(2,1)S(1)}, u32[]{:S(2)}, u32[]{:S(2)}) collective-permute-start(bf16[512,384]{1,0:T(8,128)(2,1)S(1)} %get-tuple-element.11), channel_id=1, source_target_pairs={{8,0},{12,4},{9,1},{13,5},{10,2},{14,6},{11,3},{15,7},{24,16},{28,... | collective-permute-start | bytes 1179656 | tf_op jit(solution)/shard_map/ppermute | solution.py:15
  140.8 72.8 %all-gather.14.cloned.1.call-start = ((), (), s32[]{:S(2)}) async-start(), calls=%async_computation.5 | async-start | bytes 4718592 | tf_op jit(solution)/shard_map/all_gather | solution.py:77
  164.6 3.3 %copy-start.4 = (bf16[512,1536]{1,0:T(8,128)(2,1)S(1)}, bf16[512,1536]{1,0:T(8,128)(2,1)}, u32[]{:S(2)}) copy-start(bf16[512,1536]{1,0:T(8,128)(2,1)} %param.13) | copy-start | bytes 4718596
  169.5 23.6 %all-to-all-start = ((bf16[512,2,768]{0,2,1:T(8,128)(2,1)}), bf16[512,2,768]{0,2,1:T(8,128)(2,1)S(1)}, u32[]{:S(2)}, u32[]{:S(2)}) async-start(bf16[512,2,768]{0,2,1:T(8,128)(2,1)} %bitcast.119), calls=%async_computation | async-start | bytes 3145728 | tf_op jit(solution)/shard_map/all_to_all | solution.py:100
  216.6 2.2 copy-start.6
  218.8 11.1 %copy-start.1 = (bf16[2,512,768]{2,1,0:T(8,128)(2,1)S(1)}, bf16[2,512,768]{2,1,0:T(8,128)(2,1)}, u32[]{:S(2)}) copy-start(bf16[2,512,768]{2,1,0:T(8,128)(2,1)} %copy.21) | copy-start | bytes 4718596
Sparse Core Ops, SparseCore 0:
  8.9 20.7 all-gather.5
  48.4 18.7 all-gather.7
  92.1 18.7 all-gather.9
  140.9 21.9 all-gather.11
  168.1 45.5 all-gather.13
